TPU v7x, 32 devices: a whole 2x2x4 slice. The times are simulated.
32 devices in a mesh: corpus: 4 (over z), rerank: 8 (over y, x, core).
Axes of the slice: x: 2, y: 2, z: 4, core: 2. Of those that a mesh axis runs over, the one named last changes fastest.
Arguments:
- store_rows: bfloat16 [128, 512, 3584], P('corpus', 'rerank'), may hold values from -400 to 400
- block_lengths: int32 [128], replicated, may hold values from 128 to 512
- queries: bfloat16 [32, 64, 3584], P(None, 'rerank'), may hold values from -400 to 400
- cand_owner: int32 [64, 1], replicated, may hold values from 0 to 3; in each aligned block of 16 rows (0 to 15, 16 to 31, ...) at most 5 rows name the same one
- cand_block: int32 [64], replicated, may hold values from 0 to 31
- cand_query: int32 [64], replicated, may hold values from 0 to 31
- norm_gain: bfloat16 [3584], replicated, may hold values from 0.099609375 to 1.8984375
- w_query: bfloat16 [3584, 1792], P('rerank'), may hold values from -8 to 8
- w_key: bfloat16 [3584, 256], P('rerank'), may hold values from -1 to 1
- w_value: bfloat16 [3584, 256], P('rerank'), may hold values from -0.09375 to 0.09375
- w_score: bfloat16 [1792], replicated, may hold values from -0.125 to 0.125
Outputs:
- passage_context: bfloat16 [80, 512, 1792], P('corpus', 'rerank')
- pair_scores: float32 [64], P(('corpus', 'rerank'))
Inputs may be any that keep to these rules, and one draw needn't show every extreme that they name: `cand_owner`: at most 5 of the 16 pairs of one corpus group (an aligned block of rows) name the same owner, in every draw, some group names one owner in exactly 5 of its 16 pairs.
All inputs are finite; a program needn't handle non-finite values.
Results may differ from a plain program's by a relative error of at most 0.013.
Values may be sent and summed in bfloat16 or wider, within the bound.
A program may use at most 128 MiB of HBM per device.

v0:
```python
import jax
import jax.numpy as jnp
from jax import lax
from jax.sharding import PartitionSpec as P

HDIM = 128
QHEADS = 14
KVHEADS = 2
BLK = 512
CAP = 5
ROPE_BASE = 1000000.0
EPSILON = 1e-06


def rotate(values, positions):
    head_dim = values.shape[-1]
    half_dim = head_dim // 2
    inverse = jnp.power(ROPE_BASE, -2.0 * jnp.arange(half_dim, dtype=jnp.float32) / head_dim)
    angles = positions.astype(jnp.float32)[..., None] * inverse
    cosine = jnp.cos(angles)[..., None, :]
    sine_part = jnp.sin(angles)[..., None, :]
    lower = values[..., :half_dim]
    upper = values[..., half_dim:]
    return jnp.concatenate(
        [lower * cosine - upper * sine_part, upper * cosine + lower * sine_part], axis=-1
    )


def pick_rows(table, wanted, indices):
    present = jnp.any(wanted, axis=1)
    picked = jnp.sum(jnp.where(wanted, indices[None, :], 0), axis=1)
    chosen = jnp.take(table, picked, axis=0)
    return jnp.where(present[:, None, None], chosen, jnp.zeros((), table.dtype))


def add_products(pieces, columns):
    return (
        jnp.dot(columns, pieces[0], preferred_element_type=jnp.float32),
        jnp.dot(columns, pieces[1], preferred_element_type=jnp.float32),
        jnp.dot(columns, pieces[2], preferred_element_type=jnp.float32),
    )


def attend_one(items):
    query_rot, key_rot, values, length = items
    seq_len = query_rot.shape[0]
    token_ids = jnp.arange(seq_len, dtype=jnp.int32)
    grouped = query_rot.reshape(seq_len, KVHEADS, QHEADS // KVHEADS, HDIM)
    logits = jnp.einsum(
        "skgd,tkd->kgst", grouped, key_rot, preferred_element_type=jnp.float32
    ) * HDIM ** (-0.5)
    live = (token_ids < length) | (token_ids >= BLK)
    allowed = live[None, :] & (token_ids[None, :] <= token_ids[:, None])
    masked = jnp.where(allowed, logits, -1e30)
    peak = jnp.max(masked, axis=-1, keepdims=True)
    weights = jnp.where(allowed, jnp.exp(masked - peak), 0.0)
    probs = (weights / jnp.sum(weights, axis=-1, keepdims=True)).astype(jnp.bfloat16)
    context = jnp.einsum("kgst,tkd->skgd", probs, values, preferred_element_type=jnp.float32)
    return context.reshape(seq_len, QHEADS * HDIM).astype(jnp.bfloat16)


def on_device(
    store_rows,
    block_lengths,
    queries,
    cand_owner,
    cand_block,
    cand_query,
    norm_gain,
    w_query,
    w_key,
    w_value,
    w_score,
):
    n_corpus = lax.axis_size("corpus")
    n_rerank = lax.axis_size("rerank")
    corpus_index = lax.axis_index("corpus")
    member = lax.axis_index("rerank")
    pair_total = cand_block.shape[0]
    pair_group = pair_total // n_corpus
    pair_dev = pair_group // n_rerank
    own_blocks = store_rows.shape[0]
    owners = cand_owner[:, 0]
    pair_order = jnp.arange(pair_total, dtype=jnp.int32)
    group_of = pair_order // pair_group
    earlier = (
        (owners[:, None] == owners[None, :])
        & (group_of[:, None] == group_of[None, :])
        & (pair_order[None, :] < pair_order[:, None])
    )
    owner_rank = jnp.sum(earlier.astype(jnp.int32), axis=1)
    slot_ids = jnp.arange(n_corpus * CAP, dtype=jnp.int32)
    slot_group = slot_ids // CAP
    slot_rank = slot_ids % CAP
    wanted = (
        (group_of[None, :] == slot_group[:, None])
        & (owners[None, :] == corpus_index)
        & (owner_rank[None, :] == slot_rank[:, None])
    )
    outgoing = pick_rows(store_rows, wanted, cand_block)
    arrived = lax.all_to_all(outgoing, "corpus", split_axis=0, concat_axis=0, tiled=True)
    local_pairs = corpus_index * pair_group + jnp.arange(pair_group, dtype=jnp.int32)
    local_owner = jnp.take(owners, local_pairs)
    local_rank = jnp.take(owner_rank, local_pairs)
    passages = jnp.take(arrived, local_owner * CAP + local_rank, axis=0)
    query_rows = jnp.take(queries, jnp.take(cand_query, local_pairs), axis=0)
    passage_rows, question_rows = (
        lax.all_to_all(passages, "rerank", split_axis=0, concat_axis=1, tiled=True),
        lax.all_to_all(query_rows, "rerank", split_axis=0, concat_axis=1, tiled=True),
    )
    joined = jnp.concatenate([passage_rows, question_rows], axis=1)
    device_pairs = (
        corpus_index * pair_group + member * pair_dev + jnp.arange(pair_dev, dtype=jnp.int32)
    )
    lengths = jnp.take(
        block_lengths,
        jnp.take(owners, device_pairs) * own_blocks + jnp.take(cand_block, device_pairs),
    )
    seq_len = joined.shape[1]
    width = joined.shape[2]
    row_count = pair_dev * seq_len
    widened = joined.astype(jnp.float32)
    inverse_rms = lax.rsqrt(jnp.mean(widened * widened, axis=-1, keepdims=True) + EPSILON)
    normed = (
        (widened * inverse_rms * norm_gain.astype(jnp.float32))
        .astype(jnp.bfloat16)
        .reshape(row_count, width)
    )
    query_raw, key_raw, value_raw = add_products(
        (
            lax.all_gather(w_query, "rerank", axis=0, tiled=True),
            lax.all_gather(w_key, "rerank", axis=0, tiled=True),
            lax.all_gather(w_value, "rerank", axis=0, tiled=True),
        ),
        normed,
    )
    token_ids = jnp.arange(seq_len, dtype=jnp.int32)
    positions = jnp.where(
        token_ids[None, :] < BLK, token_ids[None, :], lengths[:, None] + token_ids[None, :] - BLK
    )
    query_rot = rotate(query_raw.reshape(pair_dev, seq_len, QHEADS, HDIM), positions).astype(
        jnp.bfloat16
    )
    key_rot = rotate(key_raw.reshape(pair_dev, seq_len, KVHEADS, HDIM), positions).astype(
        jnp.bfloat16
    )
    values = value_raw.reshape(pair_dev, seq_len, KVHEADS, HDIM).astype(jnp.bfloat16)
    context = lax.map(attend_one, (query_rot, key_rot, values, lengths))
    pair_scores = jnp.dot(context[:, seq_len - 1, :], w_score, preferred_element_type=jnp.float32)
    keep = token_ids[None, :BLK] < lengths[:, None]
    passage_context = jnp.where(keep[:, :, None], context[:, :BLK], jnp.zeros((), jnp.bfloat16))
    returned = lax.all_to_all(passage_context, "rerank", split_axis=1, concat_axis=0, tiled=True)
    home_want = (local_owner[None, :] == slot_group[:, None]) & (
        local_rank[None, :] == slot_rank[:, None]
    )
    homebound = pick_rows(returned, home_want, jnp.arange(pair_group, dtype=jnp.int32))
    landed = lax.all_to_all(homebound, "corpus", split_axis=0, concat_axis=0, tiled=True)
    return (landed, pair_scores)


def solution(mesh):
    placed = (
        P("corpus", "rerank", None),
        P(),
        P(None, "rerank", None),
        P(),
        P(),
        P(),
        P(),
        P("rerank", None),
        P("rerank", None),
        P("rerank", None),
        P(),
    )
    return jax.shard_map(
        on_device,
        mesh=mesh,
        in_specs=placed,
        out_specs=(P("corpus", "rerank", None), P(("corpus", "rerank"))),
        check_vma=False,
    )
```

profile of v0, /device:TPU:2, one launch (start us, length us, event | category | flops | bytes accessed | tf_op | source)
XLA Modules:
  0.0 673.4 jit_solution(5403517321702879606)
XLA Ops:
  9.4 0.9 convert_reduce_fusion
  10.3 0.8 select_reduce_fusion
  11.4 11.1 %gather_fusion.1 = bf16[20,64,3584]{2,1,0:T(8,128)(2,1)} fusion(bf16[32,64,3584]{2,1,0:T(8,128)(2,1)} %param.17, s32[1024]{0:T(1024)S(1)} %pad_clamp_fusion.3), kind=kCustom, calls=%fused_computation.6 | custom fusion | bytes 18350160 | tf_op jit(solution)/shard_map/jit(_take)/gather | solution.py:32
  22.5 8.2 %select_select_fusion = bf16[20,64,3584]{2,1,0:T(8,128)(2,1)} fusion(bf16[20,64,3584]{2,1,0:T(8,128)(2,1)} %gather_fusion.1, pred[20]{0:T(512)(128)(4,1)S(1)} %compare_and_fusion.5, pred[20]{0:T(512)(128)(4,1)S(1)} %fusion.35), kind=kLoop, calls=%fused_computation.45 | loop fusion | flops 9175040 | bytes 18350120 | tf_op jit(solution)/shard_map/jit(_where)/select_n | solution.py:33
  30.7 5.9 all-to-all-start
  40.6 1.1 broadcast_select_fusion.2
  41.7 195.2 %all-to-all-done = bf16[20,64,3584]{2,1,0:T(8,128)(2,1)} async-done(((bf16[20,64,3584]{2,1,0:T(8,128)(2,1)}), bf16[20,64,3584]{2,1,0:T(8,128)(2,1)}, u32[]{:S(2)}, u32[]{:S(2)}) %all-to-all-start) | async-done | bytes 9175072 | tf_op jit(solution)/shard_map/all_to_all | solution.py:101
  236.8 4.2 all-to-all-start.2
  241.1 7.6 %gather_fusion.2 = bf16[16,64,3584]{2,1,0:T(8,128)(2,1)} fusion(bf16[20,64,3584]{2,1,0:T(8,128)(2,1)} %all-to-all-done, s32[1024]{0:T(1024)S(1)} %pad_clamp_fusion.2), kind=kCustom, calls=%fused_computation.7 | custom fusion | bytes 14680128 | tf_op jit(solution)/shard_map/jit(_take)/gather | solution.py:105
  248.7 6.9 %broadcast_select_fusion = bf16[16,64,3584]{2,1,0:T(8,128)(2,1)} fusion(bf16[16,64,3584]{2,1,0:T(8,128)(2,1)} %gather_fusion.2, pred[16]{0:T(512)(128)(4,1)S(1)} %get-tuple-element.63), kind=kLoop, calls=%fused_computation.50 | loop fusion | flops 3670016 | bytes 14680080 | tf_op jit(solution)/shard_map/jit(_take)/select_n | solution.py:105
  255.6 5.2 all-to-all-start.1
  263.7 2.1 multiply_cosine_fusion
  265.8 1.0 copy.62
  266.8 3.8 copy.49
  270.6 3.8 copy.48
  274.4 67.8 %all-to-all-done.1 = bf16[16,64,3584]{2,1,0:T(8,128)(2,1)} async-done(((bf16[16,64,3584]{2,1,0:T(8,128)(2,1)}), bf16[16,64,3584]{2,1,0:T(8,128)(2,1)}, u32[]{:S(2)}, u32[]{:S(2)}) %all-to-all-start.1) | async-done | bytes 7340064 | tf_op jit(solution)/shard_map/all_to_all | solution.py:108
  342.2 3.8 copy.46
  346.0 2.0 fusion.30
  348.9 2.4 fusion.41
  352.1 3.4 convolution_convert_fusion
  355.5 18.0 %copy.50 = bf16[1792,3584]{1,0:T(8,128)(2,1)} copy(bf16[1792,3584]{0,1:T(8,128)(2,1)} %bitcast.115) | data formatting | bytes 25690112 | tf_op jit(solution)/shard_map/dot_general | solution.py:38
  373.5 23.9 %fusion.39 = f32[2,576,14,128]{3,1,2,0:T(8,128)} fusion(bf16[14,128,3584,1]{2,1,0,3:T(8,128)(2,1)} %bitcast.116, f32[3584]{0:T(1024)S(1)} %convert_element_type.66, f32[2,576]{1,0:T(2,128)S(1)} %add_rsqrt_fusion, bf16[2,64,3584]{2,1,0:T(8,128)(2,1)S(1)} %bitcast.121, bf16[2,512,3584]{2,1,0:T(8,128)(2,1)} %bitcast.112), kind=kOutput, calls=%fused_computation.117 | convolution fusion | flops 14826405888 | bytes 29379072 | tf_op jit(solution)/shard_map/dot_general | solution.py:38
  397.4 8.6 %subtract_convert_fusion = (bf16[2,576,14,64]{3,1,2,0:T(8,128)(2,1)S(1)}, bf16[2,576,14,64]{3,1,2,0:T(8,128)(2,1)S(1)}) fusion(f32[2,576,14,128]{3,1,2,0:T(8,128)} %fusion.39, f32[2,576,64]{2,1,0:T(8,128)S(1)} %get-tuple-element.62, f32[2,576,64]{2,1,0:T(8,128)S(1)} %get-tuple-element.61), kind=kLoop, calls=%fused_computation.49 | loop fusion | flops 8257536 | bytes 12976128 | tf_op jit(solution)/shard_map/convert.2
  405.9 4.3 pad_maximum_fusion.1
  410.2 69.3 %while.10 = (s32[]{:T(128)}, bf16[2,576,1792]{2,1,0:T(8,128)(2,1)}, bf16[2,576,2,128]{3,1,2,0:T(8,128)(2,1)}, s32[2]{0:T(128)S(1)}, bf16[2,576,2,128]{3,1,2,0:T(...) while((s32[]{:T(128)}, bf16[2,576,1792]{2,1,0:T(8,128)(2,1)}, ...), condition=%wide.region_9.12_spmd, body=%wide.region_6.11_spmd.sunk | while | flops 2412382464 | bytes 61592804 | solution.py:148
  410.4 1.7 constant_dynamic-slice_fusion.2
  413.5 12.5 %fusion.66 = (f32[2,7,576]{2,1,0:T(8,128)S(1)}, f32[2,7,576,576]{2,3,1,0:T(8,128)}) fusion(pred[576,576]{0,1:T(8,128)(4,1)S(1)} %fusion.65, bf16[576,2,7,128]{3,0,2,1:T(8,128)(2,1)S(1)} %bitcast.108, bf16[2,576,2,128]{3,1,2,0:T(8,128)(2,1)S(1)} %get-tuple-element.128, s32[]{:T(128)} %get-tuple-element.117), kind=kOutput, calls=%fused_computation.119.clone.1 | convolution fusion | flops 1212310016 | bytes 21708292 | tf_op jit(solution)/shard_map/while/body/eval_jaxpr/sub | solution.py:56
  426.0 11.1 %convert_bitcast_fusion.2 = bf16[576,2,7,128]{3,0,2,1:T(8,128)(2,1)S(1)} fusion(f32[2,7,576,576]{2,3,1,0:T(8,128)} %get-tuple-element.108, f32[2,7,576]{2,1,0:T(8,128)S(1)} %get-tuple-element.109, bf16[2,576,2,128]{3,1,2,0:T(8,128)(2,1)} %get-tuple-element.126, s32[]{:T(128)} %get-tuple-element.117), kind=kOutput, calls=%fused_computation.19.clone.1 | convolution fusion | flops 1199407104 | bytes 23035904 | tf_op jit(solution)/shard_map/while/body/eval_jaxpr/kgst,tkd->skgd/dot_general | solution.py:58
  437.1 1.4 copy.64
  438.5 3.3 convert_element_type.102
  441.8 3.0 constant_dynamic-update-slice_fusion.2
  444.8 1.7 constant_dynamic-slice_fusion.2
  448.0 12.5 %fusion.66 = (f32[2,7,576]{2,1,0:T(8,128)S(1)}, f32[2,7,576,576]{2,3,1,0:T(8,128)}) fusion(pred[576,576]{0,1:T(8,128)(4,1)S(1)} %fusion.65, bf16[576,2,7,128]{3,0,2,1:T(8,128)(2,1)S(1)} %bitcast.108, bf16[2,576,2,128]{3,1,2,0:T(8,128)(2,1)S(1)} %get-tuple-element.128, s32[]{:T(128)} %get-tuple-element.117), kind=kOutput, calls=%fused_computation.119.clone.1 | convolution fusion | flops 1212310016 | bytes 21708292 | tf_op jit(solution)/shard_map/while/body/eval_jaxpr/sub | solution.py:56
  460.5 11.1 %convert_bitcast_fusion.2 = bf16[576,2,7,128]{3,0,2,1:T(8,128)(2,1)S(1)} fusion(f32[2,7,576,576]{2,3,1,0:T(8,128)} %get-tuple-element.108, f32[2,7,576]{2,1,0:T(8,128)S(1)} %get-tuple-element.109, bf16[2,576,2,128]{3,1,2,0:T(8,128)(2,1)} %get-tuple-element.126, s32[]{:T(128)} %get-tuple-element.117), kind=kOutput, calls=%fused_computation.19.clone.1 | convolution fusion | flops 1199407104 | bytes 23035904 | tf_op jit(solution)/shard_map/while/body/eval_jaxpr/kgst,tkd->skgd/dot_general | solution.py:58
  471.6 1.4 copy.64
  473.0 3.3 convert_element_type.102
  476.3 3.0 constant_dynamic-update-slice_fusion.2
  479.5 6.4 copy.51
  486.0 5.7 broadcast_select_fusion.1
  491.7 5.9 all-to-all-start.3
  497.8 41.8 %all-to-all-done.3 = bf16[2,512,1792]{2,0,1:T(2,128)(2,1)} async-done(((bf16[2,512,1792]{2,0,1:T(2,128)(2,1)}), bf16[2,512,1792]{2,0,1:T(2,128)(2,1)}, u32[]{:S(2)}, u32[]{:S(2)}) %all-to-all-start.3) | async-done | bytes 3670048 | tf_op jit(solution)/shard_map/all_to_all | solution.py:152
  539.7 2.5 copy.52
  542.2 2.1 copy.53
  544.3 5.3 gather_fusion.4
  549.5 5.1 select_select_fusion.1
  554.7 4.9 all-to-all-start.4
  561.1 100.6 %all-to-all-done.4 = bf16[20,64,1792]{2,1,0:T(8,128)(2,1)} async-done(((bf16[20,64,1792]{2,1,0:T(8,128)(2,1)}), bf16[20,64,1792]{2,1,0:T(8,128)(2,1)}, u32[]{:S(2)}, u32[]{:S(2)}) %all-to-all-start.4) | async-done | bytes 4587552 | tf_op jit(solution)/shard_map/all_to_all | solution.py:157
  661.8 4.9 copy.75
  (97 shorter events, 15.3 us)
Async XLA Ops:
  7.2 32.8 %copy-start = (bf16[32,8,3584]{2,1,0:T(8,128)(2,1)S(1)}, bf16[32,8,3584]{2,1,0:T(8,128)(2,1)}, u32[]{:S(2)}) copy-start(bf16[32,8,3584]{2,1,0:T(8,128)(2,1)} %param.19) | copy-start | bytes 5505028
  7.2 259.6 %all-gather.6.cloned.1.call-start = ((), (), s32[]{:S(2)}) async-start(), calls=%async_computation.6 | async-start | bytes 2064384 | tf_op jit(solution)/shard_map/all_gather | solution.py:132
  7.9 262.7 %all-gather.4.cloned.1.call-start = ((), (), s32[]{:S(2)}) async-start(), calls=%async_computation.5 | async-start | bytes 2064384 | tf_op jit(solution)/shard_map/all_gather | solution.py:133
  8.7 13.8 %copy-start.12 = (s32[20]{0:T(128)}, s32[20]{0:T(128)S(1)}, u32[]{:S(2)}) copy-start(s32[20]{0:T(128)S(1)} %get-tuple-element.67) | copy-start | bytes 244
  8.7 13.8 %copy-start.14 = (s32[20]{0:T(128)}, s32[20]{0:T(128)S(1)}, u32[]{:S(2)}) copy-start(s32[20]{0:T(128)S(1)} %get-tuple-element.68) | copy-start | bytes 244
  30.7 7.3 %copy-start.2 = (s32[64,1]{0,1:T(1,128)S(1)}, s32[64,1]{0,1:T(1,128)}, u32[]{:S(2)}) copy-start(s32[64,1]{0,1:T(1,128)} %param.20) | copy-start | bytes 772
  30.7 8.0 %copy-start.4 = (s32[64]{0:T(128)S(1)}, s32[64]{0:T(128)}, u32[]{:S(2)}) copy-start(s32[64]{0:T(128)} %param.22) | copy-start | bytes 772
  30.7 206.1 %all-to-all-start = ((bf16[20,64,3584]{2,1,0:T(8,128)(2,1)}), bf16[20,64,3584]{2,1,0:T(8,128)(2,1)}, u32[]{:S(2)}, u32[]{:S(2)}) async-start(bf16[20,64,3584]{2,1,0:T(8,128)(2,1)} %select_select_fusion), calls=%async_computation | async-start | bytes 18350080 | tf_op jit(solution)/shard_map/all_to_all | solution.py:101
  36.6 318.9 %all-gather.8.cloned.1.call-start = ((), (), s32[]{:S(2)}) async-start(), calls=%async_computation.7 | async-start | bytes 14450688 | tf_op jit(solution)/shard_map/all_gather | solution.py:131
  236.8 18.7 %all-to-all-start.2 = ((bf16[16,8,3584]{2,1,0:T(8,128)(2,1)}), bf16[16,8,3584]{2,1,0:T(8,128)(2,1)S(1)}, u32[]{:S(2)}, u32[]{:S(2)}) async-start(bf16[16,8,3584]{2,1,0:T(8,128)(2,1)} %broadcast_select_fusion.2), calls=%async_computation.2 | async-start | bytes 1835008 | tf_op jit(solution)/shard_map/all_to_all | solution.py:109
  255.6 5.9 copy-start.3
  255.6 6.6 copy-start.11
  255.6 6.6 copy-start.5
  255.6 86.6 %all-to-all-start.1 = ((bf16[16,64,3584]{2,1,0:T(8,128)(2,1)}), bf16[16,64,3584]{2,1,0:T(8,128)(2,1)}, u32[]{:S(2)}, u32[]{:S(2)}) async-start(bf16[16,64,3584]{2,1,0:T(8,128)(2,1)} %broadcast_select_fusion), calls=%async_computation.1 | async-start | bytes 14680064 | tf_op jit(solution)/shard_map/all_to_all | solution.py:108
  342.2 3.8 copy-start.7
  346.0 6.1 copy-start.6
  346.0 2.9 copy-start.9
  348.9 3.2 copy-start.8
  479.5 6.5 copy-start.10
  486.0 11.6 %copy-start.13 = (s32[20]{0:T(128)S(1)}, s32[20]{0:T(128)}, u32[]{:S(2)}) copy-start(s32[20]{0:T(128)} %copy-done.12) | copy-start | bytes 244
  486.0 11.6 %copy-start.15 = (s32[20]{0:T(128)S(1)}, s32[20]{0:T(128)}, u32[]{:S(2)}) copy-start(s32[20]{0:T(128)} %copy-done.14) | copy-start | bytes 244
  486.0 11.6 %copy-start.16 = (s32[16]{0:T(128)S(1)}, s32[16]{0:T(128)}, u32[]{:S(2)}) copy-start(s32[16]{0:T(128)} %get-tuple-element.65) | copy-start | bytes 196
  486.0 11.6 %copy-start.17 = (s32[16]{0:T(128)S(1)}, s32[16]{0:T(128)}, u32[]{:S(2)}) copy-start(s32[16]{0:T(128)} %get-tuple-element.66) | copy-start | bytes 196
  491.7 48.0 %all-to-all-start.3 = ((bf16[2,512,1792]{2,0,1:T(2,128)(2,1)}), bf16[2,512,1792]{2,0,1:T(2,128)(2,1)}, u32[]{:S(2)}, u32[]{:S(2)}) async-start(bf16[2,512,1792]{2,0,1:T(2,128)(2,1)} %broadcast_select_fusion.1), calls=%async_computation.3 | async-start | bytes 7340032 | tf_op jit(solution)/shard_map/all_to_all | solution.py:152
  549.5 10.1 %copy-start.18 = (bf16[1792]{0:T(1024)(128)(2,1)S(1)}, bf16[1792]{0:T(1024)(128)(2,1)}, u32[]{:S(2)}) copy-start(bf16[1792]{0:T(1024)(128)(2,1)} %param.27) | copy-start | bytes 10756
  549.5 117.1 %copy-start.1 = (bf16[32,8,3584]{2,1,0:T(8,128)(2,1)S(1)}, bf16[32,8,3584]{2,1,0:T(8,128)(2,1)}, u32[]{:S(2)}) copy-start(bf16[32,8,3584]{2,1,0:T(8,128)(2,1)} %param.19) | copy-start | bytes 5505028
  554.7 107.1 %all-to-all-start.4 = ((bf16[20,64,1792]{2,1,0:T(8,128)(2,1)}), bf16[20,64,1792]{2,1,0:T(8,128)(2,1)}, u32[]{:S(2)}, u32[]{:S(2)}) async-start(bf16[20,64,1792]{2,1,0:T(8,128)(2,1)} %select_select_fusion.1), calls=%async_computation.4 | async-start | bytes 9175040 | tf_op jit(solution)/shard_map/all_to_all | solution.py:157
Sparse Core Ops, SparseCore 0:
  9.9 27.8 all-gather.5
  39.7 26.6 all-gather.3
  68.3 73.0 all-gather.7
where the time goes:
time: 679 us; the launch traced here: 673 us
  waiting for transfers between devices  407 us (60%)
  local copies, waits for them, and re-layouts  96.6 us (14%)
  matrix products  77.5 us (11%)
  other arithmetic  50.7 us (7%)
  starting transfers between devices  26.3 us (4%)
  between operations  14.4 us (2%)
    all_to_all x1, waiting for transfers between devices, on_device(): lax.all_to_all(outgoing, 'corpus', split_axis=0, concat_axis=0, tiled=True)  195 us
    all_to_all x1, waiting for transfers between devices, on_device(): lax.all_to_all(homebound, 'corpus', split_axis=0, concat_axis=0, tiled=True)  101 us
    all_to_all x1, waiting for transfers between devices, on_device(): lax.all_to_all(passages, 'rerank', split_axis=0, concat_axis=1, tiled=True)  67.8 us
    all_to_all x1, waiting for transfers between devices, on_device(): lax.all_to_all(passage_context, 'rerank', split_axis=1, concat_axis=0, ti...  41.8 us
    sub x2, matrix products, attend_one(): weights = jnp.where(allowed, jnp.exp(masked - peak), 0.0)  25 us
    dot_general x1, matrix products, add_products(): jnp.dot(columns, pieces[0], preferred_element_type=jnp.float32)  23.9 us
    dot_general x2, matrix products, attend_one(): jnp.einsum('kgst,tkd->skgd', probs, values, preferred_element_type=jnp.fl...  22.2 us
    dot_general x1, local copies, waits for them, and re-layouts, add_products(): jnp.dot(columns, pieces[0], preferred_element_type=jnp.float32)  18 us
  transfers between devices with their start and end apart: 8, of which 4 were waited for; matrix products, arithmetic and copies ran while one was open for 10% of the time, Pallas kernels for 0%

commit v1 on v0

--- a/solution.py
+++ b/solution.py
@@ -10,6 +10,15 @@
 CAP = 5
 ROPE_BASE = 1000000.0
 EPSILON = 1e-06
+
+
+def _shape_indices(u, ax_name):
+    local_next = lax.axis_size(ax_name)
+    k_now = jnp.split(u, local_next, 0)
+    spare = jnp.stack(k_now, 0)
+    piece_out = lax.all_to_all(spare, ax_name, 0, 0)
+    later = jnp.concatenate(piece_out, 1)
+    return later
 
 
 def rotate(values, positions):
@@ -105,7 +114,7 @@
     passages = jnp.take(arrived, local_owner * CAP + local_rank, axis=0)
     query_rows = jnp.take(queries, jnp.take(cand_query, local_pairs), axis=0)
     passage_rows, question_rows = (
-        lax.all_to_all(passages, "rerank", split_axis=0, concat_axis=1, tiled=True),
+        _shape_indices(passages, "rerank"),
         lax.all_to_all(query_rows, "rerank", split_axis=0, concat_axis=1, tiled=True),
     )
     joined = jnp.concatenate([passage_rows, question_rows], axis=1)

time: 679 us -> 696 us (1.025)
  local copies, waits for them, and re-layouts: 96.6 us -> 105 us
  other arithmetic: 50.7 us -> 58.9 us
    another operation x2, other arithmetic: 9.03 us -> 19.2 us
    unnamed x40 -> x45, local copies, waits for them, and re-layouts: 5.8 us -> 12.9 us
  transfers between devices with their start and end apart: 8 -> 8, of which waited for: 4 -> 4; matrix products, arithmetic and copies ran while one was open for 10% -> 7% of each run, Pallas kernels for 0% -> 0%
where the time goes in v1:
time: 696 us; the launch traced here: 690 us
  waiting for transfers between devices  408 us (59%)
  local copies, waits for them, and re-layouts  105 us (15%)
  matrix products  77 us (11%)
  other arithmetic  58.9 us (8%)
  starting transfers between devices  26.4 us (4%)
  between operations  14.4 us (2%)
    all_to_all x1, waiting for transfers between devices, on_device(): lax.all_to_all(outgoing, 'corpus', split_axis=0, concat_axis=0, tiled=True)  194 us
    all_to_all x1, waiting for transfers between devices, on_device(): lax.all_to_all(homebound, 'corpus', split_axis=0, concat_axis=0, tiled=True)  101 us
    all_to_all x1, waiting for transfers between devices, _shape_indices(): piece_out = lax.all_to_all(spare, ax_name, 0, 0)  69.9 us
    all_to_all x1, waiting for transfers between devices, on_device(): lax.all_to_all(passage_context, 'rerank', split_axis=1, concat_axis=0, ti...  41.8 us
    sub x2, matrix products, attend_one(): weights = jnp.where(allowed, jnp.exp(masked - peak), 0.0)  25 us
    dot_general x1, matrix products, add_products(): jnp.dot(columns, pieces[0], preferred_element_type=jnp.float32)  23.4 us
    dot_general x2, matrix products, attend_one(): jnp.einsum('kgst,tkd->skgd', probs, values, preferred_element_type=jnp.fl...  22.2 us
    another operation x2, other arithmetic  19.2 us
  transfers between devices with their start and end apart: 8, of which 4 were waited for; matrix products, arithmetic and copies ran while one was open for 7% of the time, Pallas kernels for 0%

profile of v1, /device:TPU:2, one launch (start us, length us, event | category | flops | bytes accessed | tf_op | source)
XLA Modules:
  0.0 690.0 jit_solution(498607041915075741)
XLA Ops:
  8.1 1.3 gather_fusion.7
  9.3 1.3 gather_fusion.8
  12.6 11.1 %gather_fusion.1 = bf16[20,64,3584]{2,1,0:T(8,128)(2,1)} fusion(bf16[32,64,3584]{2,1,0:T(8,128)(2,1)} %param.17, s32[1024]{0:T(1024)S(1)} %get-tuple-element.67), kind=kCustom, calls=%fused_computation.6 | custom fusion | bytes 18350160 | tf_op jit(solution)/shard_map/jit(_take)/gather | solution.py:41
  23.7 8.2 %select_select_fusion = bf16[20,64,3584]{2,1,0:T(8,128)(2,1)} fusion(bf16[20,64,3584]{2,1,0:T(8,128)(2,1)} %gather_fusion.1, pred[20]{0:T(512)(128)(4,1)S(1)} %compare_and_fusion.5, pred[20]{0:T(512)(128)(4,1)S(1)} %fusion.43), kind=kLoop, calls=%fused_computation.45 | loop fusion | flops 9175040 | bytes 18350120 | tf_op jit(solution)/shard_map/jit(_where)/select_n | solution.py:42
  32.0 5.9 all-to-all-start
  44.4 193.7 %all-to-all-done = bf16[20,64,3584]{2,1,0:T(8,128)(2,1)} async-done(((bf16[20,64,3584]{2,1,0:T(8,128)(2,1)}), bf16[20,64,3584]{2,1,0:T(8,128)(2,1)}, u32[]{:S(2)}, u32[]{:S(2)}) %all-to-all-start) | async-done | bytes 9175072 | tf_op jit(solution)/shard_map/all_to_all | solution.py:110
  238.1 4.3 all-to-all-start.2
  242.3 7.6 %gather_fusion.2 = bf16[16,64,3584]{2,1,0:T(8,128)(2,1)} fusion(bf16[20,64,3584]{2,1,0:T(8,128)(2,1)} %all-to-all-done, s32[1024]{0:T(1024)S(1)} %pad_clamp_fusion.2), kind=kCustom, calls=%fused_computation.7 | custom fusion | bytes 14680128 | tf_op jit(solution)/shard_map/jit(_take)/gather | solution.py:114
  250.0 3.8 broadcast_select_fusion
  257.8 1.1 fusion.37
  261.9 5.3 all-to-all-start.1
  268.8 2.1 multiply_cosine_fusion
  271.0 3.8 copy.60
  274.9 3.8 copy.59
  278.7 69.9 %all-to-all-done.1 = bf16[8,2,64,3584]{3,2,1,0:T(8,128)(2,1)} async-done(((bf16[8,2,64,3584]{3,2,1,0:T(8,128)(2,1)}), bf16[8,2,64,3584]{3,2,1,0:T(8,128)(2,1)}, u32[]{:S(2)}, u32[]{:S(2)}) %all-to-all-start.1) | async-done | bytes 7340064 | tf_op jit(solution)/shard_map/all_to_all | solution.py:19
  348.6 3.7 copy.57
  352.3 2.0 fusion.30
  355.2 2.4 fusion.49
  358.1 1.2 pad_maximum_fusion.2
  359.3 3.4 convolution_convert_fusion
  362.6 17.9 %copy.61 = bf16[1792,3584]{1,0:T(8,128)(2,1)} copy(bf16[1792,3584]{0,1:T(8,128)(2,1)} %bitcast.146) | data formatting | bytes 25690112 | tf_op jit(solution)/shard_map/dot_general | solution.py:47
  380.6 23.4 %fusion.47 = f32[2,576,14,128]{3,1,2,0:T(8,128)} fusion(bf16[14,128,3584,1]{2,1,0,3:T(8,128)(2,1)} %bitcast.147, f32[3584]{0:T(1024)S(1)} %convert_element_type.66, f32[2,576]{1,0:T(2,128)S(1)} %add_rsqrt_fusion, bf16[2,64,3584]{2,1,0:T(8,128)(2,1)S(1)} %bitcast.152, bf16[2,512,3584]{2,1,0:T(8,128)(2,1)} %bitcast.143), kind=kOutput, calls=%fused_computation.133 | convolution fusion | flops 14826405888 | bytes 29379072 | tf_op jit(solution)/shard_map/dot_general | solution.py:47
  403.9 18.8 %subtract_convert_fusion = (bf16[2,576,14,64]{3,1,2,0:T(8,128)(2,1)S(1)}, bf16[2,576,14,64]{3,1,2,0:T(8,128)(2,1)S(1)}) fusion(f32[2,576,14,128]{3,1,2,0:T(8,128)} %fusion.47, f32[2,576,64]{2,1,0:T(8,128)S(1)} %get-tuple-element.62, f32[2,576,64]{2,1,0:T(8,128)S(1)} %get-tuple-element.61), kind=kLoop, calls=%fused_computation.49 | loop fusion | flops 8257536 | bytes 12976128 | tf_op jit(solution)/shard_map/convert.2
  422.7 4.3 pad_maximum_fusion.1
  427.0 69.1 %while.10 = (s32[]{:T(128)}, bf16[2,576,1792]{2,1,0:T(8,128)(2,1)}, bf16[2,576,2,128]{3,1,2,0:T(8,128)(2,1)}, s32[2]{0:T(128)S(1)}, bf16[2,576,2,128]{3,1,2,0:T(...) while((s32[]{:T(128)}, bf16[2,576,1792]{2,1,0:T(8,128)(2,1)}, ...), condition=%wide.region_9.12_spmd, body=%wide.region_6.11_spmd.sunk | while | flops 2412382464 | bytes 61592804 | solution.py:157
  427.0 1.7 constant_dynamic-slice_fusion.2
  430.2 12.5 %fusion.74 = (f32[2,7,576]{2,1,0:T(8,128)S(1)}, f32[2,7,576,576]{2,3,1,0:T(8,128)}) fusion(pred[576,576]{0,1:T(8,128)(4,1)S(1)} %fusion.73, bf16[576,2,7,128]{3,0,2,1:T(8,128)(2,1)S(1)} %bitcast.139, bf16[2,576,2,128]{3,1,2,0:T(8,128)(2,1)S(1)} %get-tuple-element.128, s32[]{:T(128)} %get-tuple-element.117), kind=kOutput, calls=%fused_computation.135.clone.1 | convolution fusion | flops 1212310016 | bytes 21708292 | tf_op jit(solution)/shard_map/while/body/eval_jaxpr/sub | solution.py:65
  442.7 11.1 %convert_bitcast_fusion.2 = bf16[576,2,7,128]{3,0,2,1:T(8,128)(2,1)S(1)} fusion(f32[2,7,576,576]{2,3,1,0:T(8,128)} %get-tuple-element.108, f32[2,7,576]{2,1,0:T(8,128)S(1)} %get-tuple-element.109, bf16[2,576,2,128]{3,1,2,0:T(8,128)(2,1)} %get-tuple-element.126, s32[]{:T(128)} %get-tuple-element.117), kind=kOutput, calls=%fused_computation.19.clone.1 | convolution fusion | flops 1199407104 | bytes 23035904 | tf_op jit(solution)/shard_map/while/body/eval_jaxpr/kgst,tkd->skgd/dot_general | solution.py:67
  453.8 1.4 copy.75
  455.1 3.3 convert_element_type.102
  458.5 3.0 constant_dynamic-update-slice_fusion.2
  461.5 1.7 constant_dynamic-slice_fusion.2
  464.7 12.5 %fusion.74 = (f32[2,7,576]{2,1,0:T(8,128)S(1)}, f32[2,7,576,576]{2,3,1,0:T(8,128)}) fusion(pred[576,576]{0,1:T(8,128)(4,1)S(1)} %fusion.73, bf16[576,2,7,128]{3,0,2,1:T(8,128)(2,1)S(1)} %bitcast.139, bf16[2,576,2,128]{3,1,2,0:T(8,128)(2,1)S(1)} %get-tuple-element.128, s32[]{:T(128)} %get-tuple-element.117), kind=kOutput, calls=%fused_computation.135.clone.1 | convolution fusion | flops 1212310016 | bytes 21708292 | tf_op jit(solution)/shard_map/while/body/eval_jaxpr/sub | solution.py:65
  477.2 11.1 %convert_bitcast_fusion.2 = bf16[576,2,7,128]{3,0,2,1:T(8,128)(2,1)S(1)} fusion(f32[2,7,576,576]{2,3,1,0:T(8,128)} %get-tuple-element.108, f32[2,7,576]{2,1,0:T(8,128)S(1)} %get-tuple-element.109, bf16[2,576,2,128]{3,1,2,0:T(8,128)(2,1)} %get-tuple-element.126, s32[]{:T(128)} %get-tuple-element.117), kind=kOutput, calls=%fused_computation.19.clone.1 | convolution fusion | flops 1199407104 | bytes 23035904 | tf_op jit(solution)/shard_map/while/body/eval_jaxpr/kgst,tkd->skgd/dot_general | solution.py:67
  488.3 1.4 copy.75
  489.7 3.3 convert_element_type.102
  493.0 3.0 constant_dynamic-update-slice_fusion.2
  496.0 6.4 copy.62
  502.5 5.7 broadcast_select_fusion.1
  508.2 5.9 all-to-all-start.3
  514.4 41.8 %all-to-all-done.3 = bf16[2,512,1792]{2,0,1:T(2,128)(2,1)} async-done(((bf16[2,512,1792]{2,0,1:T(2,128)(2,1)}), bf16[2,512,1792]{2,0,1:T(2,128)(2,1)}, u32[]{:S(2)}, u32[]{:S(2)}) %all-to-all-start.3) | async-done | bytes 3670048 | tf_op jit(solution)/shard_map/all_to_all | solution.py:161
  556.3 2.5 copy.63
  558.7 2.1 copy.64
  560.8 5.3 gather_fusion.4
  566.1 5.1 select_select_fusion.1
  571.3 4.9 all-to-all-start.4
  577.7 100.6 %all-to-all-done.4 = bf16[20,64,1792]{2,1,0:T(8,128)(2,1)} async-done(((bf16[20,64,1792]{2,1,0:T(8,128)(2,1)}), bf16[20,64,1792]{2,1,0:T(8,128)(2,1)}, u32[]{:S(2)}, u32[]{:S(2)}) %all-to-all-start.4) | async-done | bytes 4587552 | tf_op jit(solution)/shard_map/all_to_all | solution.py:166
  678.3 4.9 copy.93
  (103 shorter events, 23.9 us)
Async XLA Ops:
  7.2 35.5 %copy-start = (bf16[32,8,3584]{2,1,0:T(8,128)(2,1)S(1)}, bf16[32,8,3584]{2,1,0:T(8,128)(2,1)}, u32[]{:S(2)}) copy-start(bf16[32,8,3584]{2,1,0:T(8,128)(2,1)} %param.19) | copy-start | bytes 5505028
  7.2 16.5 %copy-start.11 = (s32[20]{0:T(128)}, s32[20]{0:T(128)S(1)}, u32[]{:S(2)}) copy-start(s32[20]{0:T(128)S(1)} %and_select_fusion.1) | copy-start | bytes 244
  7.2 16.5 %copy-start.13 = (s32[20]{0:T(128)}, s32[20]{0:T(128)S(1)}, u32[]{:S(2)}) copy-start(s32[20]{0:T(128)S(1)} %and_select_fusion.3) | copy-start | bytes 244
  32.0 8.8 %copy-start.2 = (s32[64,1]{0,1:T(1,128)S(1)}, s32[64,1]{0,1:T(1,128)}, u32[]{:S(2)}) copy-start(s32[64,1]{0,1:T(1,128)} %param.20) | copy-start | bytes 772
  32.0 9.4 %copy-start.3 = (s32[64]{0:T(128)S(1)}, s32[64]{0:T(128)}, u32[]{:S(2)}) copy-start(s32[64]{0:T(128)} %param.22) | copy-start | bytes 772
  32.0 206.1 %all-to-all-start = ((bf16[20,64,3584]{2,1,0:T(8,128)(2,1)}), bf16[20,64,3584]{2,1,0:T(8,128)(2,1)}, u32[]{:S(2)}, u32[]{:S(2)}) async-start(bf16[20,64,3584]{2,1,0:T(8,128)(2,1)} %select_select_fusion), calls=%async_computation | async-start | bytes 18350080 | tf_op jit(solution)/shard_map/all_to_all | solution.py:110
  37.8 233.2 %all-gather.6.cloned.1.call-start = ((), (), s32[]{:S(2)}) async-start(), calls=%async_computation.6 | async-start | bytes 2064384 | tf_op jit(solution)/shard_map/all_gather | solution.py:141
  38.6 236.3 %all-gather.4.cloned.1.call-start = ((), (), s32[]{:S(2)}) async-start(), calls=%async_computation.5 | async-start | bytes 2064384 | tf_op jit(solution)/shard_map/all_gather | solution.py:142
  39.3 323.3 %all-gather.8.cloned.1.call-start = ((), (), s32[]{:S(2)}) async-start(), calls=%async_computation.7 | async-start | bytes 14450688 | tf_op jit(solution)/shard_map/all_gather | solution.py:140
  238.1 23.9 %all-to-all-start.2 = ((bf16[16,8,3584]{2,1,0:T(8,128)(2,1)}), bf16[16,8,3584]{2,1,0:T(8,128)(2,1)S(1)}, u32[]{:S(2)}, u32[]{:S(2)}) async-start(bf16[16,8,3584]{2,1,0:T(8,128)(2,1)} %broadcast_select_fusion.2), calls=%async_computation.2 | async-start | bytes 1835008 | tf_op jit(solution)/shard_map/all_to_all | solution.py:118
  261.9 5.3 copy-start.10
  261.9 5.4 copy-start.4
  261.9 86.7 %all-to-all-start.1 = ((bf16[8,2,64,3584]{3,2,1,0:T(8,128)(2,1)}), bf16[8,2,64,3584]{3,2,1,0:T(8,128)(2,1)}, u32[]{:S(2)}, u32[]{:S(2)}) async-start(bf16[8,2,64,3584]{3,2,1,0:T(8,128)(2,1)} %fusion.34), calls=%async_computation.1 | async-start | bytes 14680064 | tf_op jit(solution)/shard_map/all_to_all | solution.py:19
  352.3 6.9 %copy-start.5 = (bf16[8,2,64,3584]{3,2,0,1:T(8,128)(2,1)}, bf16[8,2,64,3584]{3,2,0,1:T(8,128)(2,1)S(1)}, u32[]{:S(2)}) copy-start(bf16[8,2,64,3584]{3,2,0,1:T(8,128)(2,1)S(1)} %copy.57) | copy-start | bytes 22020100
  352.3 2.9 copy-start.7
  355.2 4.1 copy-start.6
  422.7 4.3 copy-start.8
  496.0 6.5 copy-start.9
  502.5 11.7 %copy-start.12 = (s32[20]{0:T(128)S(1)}, s32[20]{0:T(128)}, u32[]{:S(2)}) copy-start(s32[20]{0:T(128)} %copy-done.11) | copy-start | bytes 244
  502.5 11.7 %copy-start.14 = (s32[20]{0:T(128)S(1)}, s32[20]{0:T(128)}, u32[]{:S(2)}) copy-start(s32[20]{0:T(128)} %copy-done.13) | copy-start | bytes 244
  502.5 11.7 %copy-start.15 = (s32[16]{0:T(128)S(1)}, s32[16]{0:T(128)}, u32[]{:S(2)}) copy-start(s32[16]{0:T(128)} %get-tuple-element.65) | copy-start | bytes 196
  502.5 11.7 %copy-start.16 = (s32[16]{0:T(128)S(1)}, s32[16]{0:T(128)}, u32[]{:S(2)}) copy-start(s32[16]{0:T(128)} %get-tuple-element.66) | copy-start | bytes 196
  508.2 48.0 %all-to-all-start.3 = ((bf16[2,512,1792]{2,0,1:T(2,128)(2,1)}), bf16[2,512,1792]{2,0,1:T(2,128)(2,1)}, u32[]{:S(2)}, u32[]{:S(2)}) async-start(bf16[2,512,1792]{2,0,1:T(2,128)(2,1)} %broadcast_select_fusion.1), calls=%async_computation.3 | async-start | bytes 7340032 | tf_op jit(solution)/shard_map/all_to_all | solution.py:161
  566.1 10.1 %copy-start.17 = (bf16[1792]{0:T(1024)(128)(2,1)S(1)}, bf16[1792]{0:T(1024)(128)(2,1)}, u32[]{:S(2)}) copy-start(bf16[1792]{0:T(1024)(128)(2,1)} %param.27) | copy-start | bytes 10756
  566.1 117.1 %copy-start.1 = (bf16[32,8,3584]{2,1,0:T(8,128)(2,1)S(1)}, bf16[32,8,3584]{2,1,0:T(8,128)(2,1)}, u32[]{:S(2)}) copy-start(bf16[32,8,3584]{2,1,0:T(8,128)(2,1)} %param.19) | copy-start | bytes 5505028
  571.3 107.1 %all-to-all-start.4 = ((bf16[20,64,1792]{2,1,0:T(8,128)(2,1)}), bf16[20,64,1792]{2,1,0:T(8,128)(2,1)}, u32[]{:S(2)}, u32[]{:S(2)}) async-start(bf16[20,64,1792]{2,1,0:T(8,128)(2,1)} %select_select_fusion.1), calls=%async_computation.4 | async-start | bytes 9175040 | tf_op jit(solution)/shard_map/all_to_all | solution.py:166
Sparse Core Ops, SparseCore 0:
  40.5 28.0 all-gather.5
  70.5 26.6 all-gather.3
  99.1 73.0 all-gather.7
